TPU v7x, 512 devices: a whole 4x8x8 slice. The times are simulated.
512 devices in a mesh: dev: 32 (over y_hi, z), ha: 2 (over y_lo), col: 8 (over x, core).
Axes of the slice: x: 4, y: 8 (y_hi: 4, y_lo: 2; y = y_hi * 2 + y_lo), z: 8, core: 2. Of those that a mesh axis runs over, the one named last changes fastest.
Arguments:
- features: bfloat16 [128, 128, 32, 128], P('col', 'dev', 'ha'), may hold values from -6 to 6
- kernel: bfloat16 [3, 3, 3, 128, 128], P(None, None, None, 'col'), may hold values from -0.109375 to 0.109375
- channel_bias: float32 [128], P('col'), may hold values from -3 to 3
Outputs:
- activated: bfloat16 [128, 128, 32, 128], P('col', 'dev', 'ha')
All inputs are finite; a program needn't handle non-finite values.
Results may differ from a plain program's by a relative error of at most 0.005.
Values may be sent and summed in bfloat16 or wider, within the bound.
A program may use at most 64 MiB of HBM per device.

v0:
```python
import jax
import jax.numpy as jnp
from jax import lax
from jax.sharding import PartitionSpec as P


def with_halo(x, sides, width):
    for axis, dim in sides:
        devices, length = (lax.axis_size(axis), x.shape[dim])
        up = [(i, (i + 1) % devices) for i in range(devices - 1)]
        down = [(j, i) for i, j in up]
        last = lax.slice_in_dim(x, length - width, length, axis=dim)
        first = lax.slice_in_dim(x, 0, width, axis=dim)
        before = lax.ppermute(last, axis, up)
        after = lax.ppermute(first, axis, down)
        x = jnp.concatenate([before, x, after], axis=dim)
    return x


def convolve(padded, weights):
    depth_pad = padded.shape[1]
    height_pad = padded.shape[2]
    width_cells = padded.shape[3]
    outer = weights.shape[3]
    depth_cells = depth_pad - 2
    height_cells = height_pad - 2
    partial_sums = [
        jnp.zeros((outer, depth_cells, height_cells, width_cells), jnp.float32)
        for col_tap in range(3)
    ]
    for depth_tap in range(3):
        planes = padded[:, depth_tap : depth_tap + depth_cells]
        tap_out = lax.dot_general(
            weights[depth_tap], planes, (((3,), (0,)), ((), ())), preferred_element_type=jnp.float32
        )
        for row_tap in range(3):
            for col_tap in range(3):
                partial_sums[col_tap] = (
                    partial_sums[col_tap]
                    + tap_out[row_tap, col_tap, :, :, row_tap : row_tap + height_cells, :]
                )
    zero_column = jnp.zeros((outer, depth_cells, height_cells, 1), jnp.float32)
    from_left = jnp.concatenate([zero_column, partial_sums[0][..., :-1]], axis=3)
    from_right = jnp.concatenate([partial_sums[2][..., 1:], zero_column], axis=3)
    return partial_sums[1] + from_left + from_right


def finish(summed, offsets):
    summed = summed + offsets[:, None, None, None]
    return jnp.where(summed >= 0, summed, 0.3 * summed).astype(jnp.bfloat16)


def per_device(features, kernel, channel_bias):
    padded = with_halo(features, (("dev", 1), ("ha", 2)), 1)
    gathered = lax.all_gather(padded, "col", axis=0, tiled=True)
    return finish(convolve(gathered, kernel), channel_bias)


def solution(mesh):
    in_specs = (P("col", "dev", "ha", None), P(None, None, None, "col", None), P("col"))
    out_specs = P("col", "dev", "ha", None)
    return jax.shard_map(
        per_device, mesh=mesh, in_specs=in_specs, out_specs=out_specs, check_vma=False
    )
```

profile of v0, /device:TPU:1, one launch (start us, length us, event | category | flops | bytes accessed | tf_op | source)
XLA Modules:
  0.0 85.2 jit_solution(9481461446292273636)
XLA Ops:
  6.5 0.0 all-gather.2.cloned.1.call-start
  6.5 0.9 %fusion.24 = (bf16[16,1,16,128]{3,2,1,0:T(8,128)(2,1)S(1)}, bf16[16,1,16,128]{3,2,1,0:T(8,128)(2,1)S(1)}) fusion(bf16[16,4,16,128]{3,2,1,0:T(8,128)(2,1)} %param.3), kind=kLoop, calls=%fused_computation.61 | loop fusion | bytes 262144 | tf_op jit(solution)/shard_map/slice | solution.py:13
  7.5 4.8 %collective-permute-start = (bf16[16,1,16,128]{3,0,2,1:T(8,128)(2,1)S(1)}, bf16[16,1,16,128]{3,0,2,1:T(8,128)(2,1)S(1)}, u32[]{:S(2)}, u32[]{:S(2)}) collective-permute-start(bf16[16,1,16,128]{3,0,2,1:T(8,128)(2,1)S(1)} %copy.37), channel_id=1, source_target_pairs={{0,16},{16,32},{32,48},{48,64},{64,80},{80,96},{96,112},{112,128},... | collective-permute-start | bytes 196616 | tf_op jit(solution)/shard_map/ppermute | solution.py:14
  12.3 1.3 %collective-permute-start.1 = (bf16[16,1,16,128]{3,0,2,1:T(8,128)(2,1)S(1)}, bf16[16,1,16,128]{3,0,2,1:T(8,128)(2,1)S(1)}, u32[]{:S(2)}, u32[]{:S(2)}) collective-permute-start(bf16[16,1,16,128]{3,0,2,1:T(8,128)(2,1)S(1)} %copy.38), channel_id=1, source_target_pairs={{16,0},{32,16},{48,32},{64,48},{80,64},{96,80},{112,96},{128,112},... | collective-permute-start | bytes 196616 | tf_op jit(solution)/shard_map/ppermute | solution.py:15
  13.6 0.0 collective-permute-done
  13.6 1.1 %constant_dynamic-update-slice_fusion.1 = bf16[16,6,16,128]{3,0,2,1:T(8,128)(2,1)S(1)} fusion(bf16[16,6,16,128]{3,0,2,1:T(8,128)(2,1)S(1)} %constant_dynamic-update-slice_fusion.2, bf16[16,4,16,128]{3,2,1,0:T(8,128)(2,1)} %param.3), kind=kLoop, calls=%fused_computation.58 | loop fusion | bytes 524288
  14.8 3.2 %collective-permute-done.1 = bf16[16,1,16,128]{3,0,2,1:T(8,128)(2,1)S(1)} collective-permute-done((bf16[16,1,16,128]{3,0,2,1:T(8,128)(2,1)S(1)}, bf16[16,1,16,128]{3,0,2,1:T(8,128)(2,1)S(1)}, u32[]{:S(2)}, u32[]{:S(2)}) %collective-permute-start.1) | collective-permute-done | bytes 65568 | tf_op jit(solution)/shard_map/ppermute | solution.py:15
  18.0 3.2 %collective-permute-start.2 = (bf16[16,6,1,128]{3,0,2,1:T(8,128)(2,1)S(1)}, bf16[16,6,1,128]{3,0,2,1:T(8,128)(2,1)S(1)}, u32[]{:S(2)}, u32[]{:S(2)}) collective-permute-start(bf16[16,6,1,128]{3,0,2,1:T(8,128)(2,1)S(1)} %get-tuple-element.5), channel_id=1, source_target_pairs={{0,8},{1,9},{2,10},{3,11},{4,12},{5,13},{6,14},{7,15},{16,24},{17,... | collective-permute-start | bytes 73736 | tf_op jit(solution)/shard_map/ppermute | solution.py:14
  21.2 1.3 %collective-permute-start.3 = (bf16[16,6,1,128]{3,0,2,1:T(8,128)(2,1)S(1)}, bf16[16,6,1,128]{3,0,2,1:T(8,128)(2,1)S(1)}, u32[]{:S(2)}, u32[]{:S(2)}) collective-permute-start(bf16[16,6,1,128]{3,0,2,1:T(8,128)(2,1)S(1)} %get-tuple-element.6), channel_id=1, source_target_pairs={{8,0},{9,1},{10,2},{11,3},{12,4},{13,5},{14,6},{15,7},{24,16},{25,... | collective-permute-start | bytes 73736 | tf_op jit(solution)/shard_map/ppermute | solution.py:15
  22.5 0.0 collective-permute-done.2
  22.5 3.3 %collective-permute-done.3 = bf16[16,6,1,128]{3,0,2,1:T(8,128)(2,1)S(1)} collective-permute-done((bf16[16,6,1,128]{3,0,2,1:T(8,128)(2,1)S(1)}, bf16[16,6,1,128]{3,0,2,1:T(8,128)(2,1)S(1)}, u32[]{:S(2)}, u32[]{:S(2)}) %collective-permute-start.3) | collective-permute-done | bytes 24608 | tf_op jit(solution)/shard_map/ppermute | solution.py:15
  25.8 0.8 pad_maximum_fusion
  26.6 0.0 all-gather.2.cloned.1.call-update
  26.7 0.0 copy-start.1
  26.7 45.2 %all-gather.2.cloned.1.call-done = bf16[128,6,18,128]{3,0,2,1:T(8,128)(2,1)} async-done(((bf16[16,6,18,128]{3,0,2,1:T(8,128)(2,1)}), bf16[128,6,18,128]{3,0,2,1:T(8,128)(2,1)}) %all-gather.2.cloned.1.call-update) | async-done | bytes 3538960 | tf_op jit(solution)/shard_map/all_gather | solution.py:55
  71.9 0.0 copy-start
  71.9 2.7 %convolution_bitcast_fusion = f32[3,3,16,4,18,128]{5,2,4,3,1,0:T(8,128)S(1)} fusion(bf16[128,6,18,128]{3,0,2,1:T(8,128)(2,1)} %all-gather.2.cloned.1.call-done, bf16[3,3,3,16,128]{4,3,2,1,0:T(8,128)(2,1)} %param.4), kind=kOutput, calls=%fused_computation | convolution fusion | flops 339738624 | bytes 7704576 | tf_op jit(solution)/shard_map/dot_general | solution.py:33
  74.6 0.0 copy-done.1
  74.6 0.1 copy-done
  74.6 0.8 convolution_bitcast_fusion.1
  75.5 0.8 convolution_bitcast_fusion.2
  76.3 0.0 copy-start.2
  76.3 0.3 fusion.2
  76.7 0.3 fusion.8
  77.0 0.2 slice.191
  77.2 0.0 copy-done.2
  77.2 0.4 fusion
  77.6 0.8 copy.21
  (5 shorter events, 0.1 us)
Async XLA Ops:
  6.5 65.4 %all-gather.2.cloned.1.call-start = ((), (), s32[]{:S(2)}) async-start(), calls=%async_computation | async-start | bytes 3981312 | tf_op jit(solution)/shard_map/all_gather | solution.py:55
  7.5 6.2 %collective-permute-start = (bf16[16,1,16,128]{3,0,2,1:T(8,128)(2,1)S(1)}, bf16[16,1,16,128]{3,0,2,1:T(8,128)(2,1)S(1)}, u32[]{:S(2)}, u32[]{:S(2)}) collective-permute-start(bf16[16,1,16,128]{3,0,2,1:T(8,128)(2,1)S(1)} %copy.37), channel_id=1, source_target_pairs={{0,16},{16,32},{32,48},{48,64},{64,80},{80,96},{96,112},{112,128},... | collective-permute-start | bytes 196616 | tf_op jit(solution)/shard_map/ppermute | solution.py:14
  12.3 5.6 %collective-permute-start.1 = (bf16[16,1,16,128]{3,0,2,1:T(8,128)(2,1)S(1)}, bf16[16,1,16,128]{3,0,2,1:T(8,128)(2,1)S(1)}, u32[]{:S(2)}, u32[]{:S(2)}) collective-permute-start(bf16[16,1,16,128]{3,0,2,1:T(8,128)(2,1)S(1)} %copy.38), channel_id=1, source_target_pairs={{16,0},{32,16},{48,32},{64,48},{80,64},{96,80},{112,96},{128,112},... | collective-permute-start | bytes 196616 | tf_op jit(solution)/shard_map/ppermute | solution.py:15
  18.0 4.5 %collective-permute-start.2 = (bf16[16,6,1,128]{3,0,2,1:T(8,128)(2,1)S(1)}, bf16[16,6,1,128]{3,0,2,1:T(8,128)(2,1)S(1)}, u32[]{:S(2)}, u32[]{:S(2)}) collective-permute-start(bf16[16,6,1,128]{3,0,2,1:T(8,128)(2,1)S(1)} %get-tuple-element.5), channel_id=1, source_target_pairs={{0,8},{1,9},{2,10},{3,11},{4,12},{5,13},{6,14},{7,15},{16,24},{17,... | collective-permute-start | bytes 73736 | tf_op jit(solution)/shard_map/ppermute | solution.py:14
  21.2 4.6 %collective-permute-start.3 = (bf16[16,6,1,128]{3,0,2,1:T(8,128)(2,1)S(1)}, bf16[16,6,1,128]{3,0,2,1:T(8,128)(2,1)S(1)}, u32[]{:S(2)}, u32[]{:S(2)}) collective-permute-start(bf16[16,6,1,128]{3,0,2,1:T(8,128)(2,1)S(1)} %get-tuple-element.6), channel_id=1, source_target_pairs={{8,0},{9,1},{10,2},{11,3},{12,4},{13,5},{14,6},{15,7},{24,16},{25,... | collective-permute-start | bytes 73736 | tf_op jit(solution)/shard_map/ppermute | solution.py:15
  26.7 47.9 %copy-start.1 = (bf16[3,3,3,16,128]{4,3,2,1,0:T(8,128)(2,1)S(1)}, bf16[3,3,3,16,128]{4,3,2,1,0:T(8,128)(2,1)}, u32[]{:S(2)}) copy-start(bf16[3,3,3,16,128]{4,3,2,1,0:T(8,128)(2,1)} %param.4) | copy-start | bytes 331780
  71.9 2.7 %copy-start = (bf16[128,6,18,128]{3,0,2,1:T(8,128)(2,1)S(1)}, bf16[128,6,18,128]{3,0,2,1:T(8,128)(2,1)}, u32[]{:S(2)}) copy-start(bf16[128,6,18,128]{3,0,2,1:T(8,128)(2,1)} %all-gather.2.cloned.1.call-done) | copy-start | bytes 10616836
  76.3 0.8 copy-start.2
Sparse Core Ops, SparseCore 0:
  26.8 45.0 all-gather.1
where the time goes:
time: 85.4 us; the launch traced here: 85.2 us
  waiting for transfers between devices  51.7 us (61%)
  between operations  13.5 us (16%)
  starting transfers between devices  10.6 us (12%)
  matrix products  4.34 us (5%)
  local copies, waits for them, and re-layouts  3.13 us (4%)
  other arithmetic  1.86 us (2%)
    all_gather x1, waiting for transfers between devices, per_device(): gathered = lax.all_gather(padded, 'col', axis=0, tiled=True)  45.2 us
    ppermute x2, starting transfers between devices, with_halo(): before = lax.ppermute(last, axis, up)  8.02 us
    ppermute x2, waiting for transfers between devices, with_halo(): after = lax.ppermute(first, axis, down)  6.47 us
    dot_general x3, matrix products, convolve(): lax.dot_general(weights[depth_tap], planes, (((3,), (0,)), ((), ())), pre...  4.34 us
    ppermute x2, starting transfers between devices, with_halo(): after = lax.ppermute(first, axis, down)  2.58 us
  transfers between devices with their start and end apart: 5, of which 3 were waited for; matrix products, arithmetic and copies ran while one was open for 1% of the time, Pallas kernels for 0%

commit v1 on v0

--- a/solution.py
+++ b/solution.py
@@ -2,6 +2,28 @@
 import jax.numpy as jnp
 from jax import lax
 from jax.sharding import PartitionSpec as P
+from jax.lax import axis_index, axis_size, ppermute
+
+
+def post_wires(message):
+    row_axis = "col"
+    cores_n = axis_size(row_axis)
+    crops = []
+    for ii in [*range(cores_n)]:
+        crops.append((ii, (ii + 1) % cores_n))
+    stack_in = []
+    for ii in tuple(range(cores_n)):
+        stack_in.append((ii, (ii - 1) % cores_n))
+    taken_in, field_out = ([message], [message])
+    for _ in range(cores_n // 2):
+        taken_in.append(ppermute(taken_in[-1], perm=crops, axis_name=row_axis))
+    for _ in tuple(range((cores_n - 1) // 2)):
+        field_out.append(ppermute(field_out[-1], axis_name=row_axis, perm=stack_in))
+    return jnp.roll(
+        jnp.concatenate([*taken_in[::-1], *field_out[1:]], axis=0),
+        (axis_index(row_axis) - cores_n // 2) * message.shape[0],
+        axis=0,
+    )
 
 
 def with_halo(x, sides, width):
@@ -52,7 +74,7 @@
 
 def per_device(features, kernel, channel_bias):
     padded = with_halo(features, (("dev", 1), ("ha", 2)), 1)
-    gathered = lax.all_gather(padded, "col", axis=0, tiled=True)
+    gathered = post_wires(padded)
     return finish(convolve(gathered, kernel), channel_bias)
 
 

time: 85.4 us -> 68.4 us (0.80)
  the two profiles are of different devices: /device:TPU:1 before, /device:TPU:55 now
where the time goes in v1:
time: 68.4 us; the launch traced here: 68.2 us
  starting transfers between devices  31 us (45%)
  waiting for transfers between devices  28.9 us (42%)
  local copies, waits for them, and re-layouts  4.19 us (6%)
  matrix products  2.54 us (4%)
  other arithmetic  1.24 us (2%)
    ppermute x4, waiting for transfers between devices, post_wires(): taken_in.append(ppermute(taken_in[-1], perm=crops, axis_name=row_axis))  21 us
    ppermute x4, starting transfers between devices, post_wires(): taken_in.append(ppermute(taken_in[-1], perm=crops, axis_name=row_axis))  14.3 us
    ppermute x2, starting transfers between devices, with_halo(): after = lax.ppermute(first, axis, down)  11.5 us
    ppermute x2, starting transfers between devices, with_halo(): before = lax.ppermute(last, axis, up)  5.29 us
    ppermute x2, waiting for transfers between devices, with_halo(): after = lax.ppermute(first, axis, down)  4.81 us
    ppermute x3, waiting for transfers between devices, post_wires(): field_out.append(ppermute(field_out[-1], axis_name=row_axis, perm=stack_in))  3.1 us
    dot_general x3, matrix products, convolve(): lax.dot_general(weights[depth_tap], planes, (((3,), (0,)), ((), ())), pre...  2.54 us
    unnamed x21, local copies, waits for them, and re-layouts  2.23 us
  transfers between devices with their start and end apart: 11, of which 7 were waited for; matrix products, arithmetic and copies ran while one was open for 3% of the time, Pallas kernels for 0%

profile of v1, /device:TPU:55, one launch (start us, length us, event | category | flops | bytes accessed | tf_op | source)
XLA Modules:
  0.0 68.2 jit_solution(5121690138902713716)
XLA Ops:
  0.0 0.9 %fusion.27 = (bf16[16,1,16,128]{3,2,1,0:T(8,128)(2,1)S(1)}, bf16[16,1,16,128]{3,2,1,0:T(8,128)(2,1)S(1)}) fusion(bf16[16,4,16,128]{3,2,1,0:T(8,128)(2,1)} %param.3), kind=kLoop, calls=%fused_computation.80 | loop fusion | bytes 262144 | tf_op jit(solution)/shard_map/slice | solution.py:35
  0.9 4.0 %collective-permute-start = (bf16[16,1,16,128]{3,0,2,1:T(8,128)(2,1)S(1)}, bf16[16,1,16,128]{3,0,2,1:T(8,128)(2,1)S(1)}, u32[]{:S(2)}, u32[]{:S(2)}) collective-permute-start(bf16[16,1,16,128]{3,0,2,1:T(8,128)(2,1)S(1)} %copy.37), channel_id=1, source_target_pairs={{0,16},{16,32},{32,48},{48,64},{64,80},{80,96},{96,112},{112,128},... | collective-permute-start | bytes 196616 | tf_op jit(solution)/shard_map/ppermute | solution.py:36
  4.9 10.2 %collective-permute-start.1 = (bf16[16,1,16,128]{3,0,2,1:T(8,128)(2,1)S(1)}, bf16[16,1,16,128]{3,0,2,1:T(8,128)(2,1)S(1)}, u32[]{:S(2)}, u32[]{:S(2)}) collective-permute-start(bf16[16,1,16,128]{3,0,2,1:T(8,128)(2,1)S(1)} %copy.38), channel_id=1, source_target_pairs={{16,0},{32,16},{48,32},{64,48},{80,64},{96,80},{112,96},{128,112},... | collective-permute-start | bytes 196616 | tf_op jit(solution)/shard_map/ppermute | solution.py:37
  15.1 0.0 collective-permute-done
  15.1 1.1 %constant_dynamic-update-slice_fusion.1 = bf16[16,6,16,128]{3,0,2,1:T(8,128)(2,1)S(1)} fusion(bf16[16,6,16,128]{3,0,2,1:T(8,128)(2,1)S(1)} %constant_dynamic-update-slice_fusion.2, bf16[16,4,16,128]{3,2,1,0:T(8,128)(2,1)} %param.3), kind=kLoop, calls=%fused_computation.52 | loop fusion | bytes 524288
  16.3 1.6 %collective-permute-done.1 = bf16[16,1,16,128]{3,0,2,1:T(8,128)(2,1)S(1)} collective-permute-done((bf16[16,1,16,128]{3,0,2,1:T(8,128)(2,1)S(1)}, bf16[16,1,16,128]{3,0,2,1:T(8,128)(2,1)S(1)}, u32[]{:S(2)}, u32[]{:S(2)}) %collective-permute-start.1) | collective-permute-done | bytes 65568 | tf_op jit(solution)/shard_map/ppermute | solution.py:37
  17.9 1.3 %collective-permute-start.2 = (bf16[16,6,1,128]{3,0,2,1:T(8,128)(2,1)S(1)}, bf16[16,6,1,128]{3,0,2,1:T(8,128)(2,1)S(1)}, u32[]{:S(2)}, u32[]{:S(2)}) collective-permute-start(bf16[16,6,1,128]{3,0,2,1:T(8,128)(2,1)S(1)} %get-tuple-element.5), channel_id=1, source_target_pairs={{0,8},{1,9},{2,10},{3,11},{4,12},{5,13},{6,14},{7,15},{16,24},{17,... | collective-permute-start | bytes 73736 | tf_op jit(solution)/shard_map/ppermute | solution.py:36
  19.2 1.3 %collective-permute-start.3 = (bf16[16,6,1,128]{3,0,2,1:T(8,128)(2,1)S(1)}, bf16[16,6,1,128]{3,0,2,1:T(8,128)(2,1)S(1)}, u32[]{:S(2)}, u32[]{:S(2)}) collective-permute-start(bf16[16,6,1,128]{3,0,2,1:T(8,128)(2,1)S(1)} %get-tuple-element.6), channel_id=1, source_target_pairs={{8,0},{9,1},{10,2},{11,3},{12,4},{13,5},{14,6},{15,7},{24,16},{25,... | collective-permute-start | bytes 73736 | tf_op jit(solution)/shard_map/ppermute | solution.py:37
  20.5 0.0 collective-permute-done.2
  20.5 3.3 %collective-permute-done.3 = bf16[16,6,1,128]{3,0,2,1:T(8,128)(2,1)S(1)} collective-permute-done((bf16[16,6,1,128]{3,0,2,1:T(8,128)(2,1)S(1)}, bf16[16,6,1,128]{3,0,2,1:T(8,128)(2,1)S(1)}, u32[]{:S(2)}, u32[]{:S(2)}) %collective-permute-start.3) | collective-permute-done | bytes 24608 | tf_op jit(solution)/shard_map/ppermute | solution.py:37
  23.7 0.1 pad_maximum_fusion
  23.8 3.2 %collective-permute-start.4 = (bf16[16,6,18,128]{3,0,2,1:T(8,128)(2,1)S(1)}, bf16[16,6,18,128]{3,0,2,1:T(8,128)(2,1)S(1)}, u32[]{:S(2)}, u32[]{:S(2)}) collective-permute-start(bf16[16,6,18,128]{3,0,2,1:T(8,128)(2,1)S(1)} %pad_maximum_fusion), channel_id=1, source_target_pairs={{0,1},{1,2},{2,3},{3,4},{4,5},{5,6},{6,7},{7,0},{8,9},{9,10},{10,1... | collective-permute-start | bytes 1327112 | tf_op jit(solution)/shard_map/ppermute | solution.py:19
  27.0 5.2 %collective-permute-done.4 = bf16[16,6,18,128]{3,0,2,1:T(8,128)(2,1)S(1)} collective-permute-done((bf16[16,6,18,128]{3,0,2,1:T(8,128)(2,1)S(1)}, bf16[16,6,18,128]{3,0,2,1:T(8,128)(2,1)S(1)}, u32[]{:S(2)}, u32[]{:S(2)}) %collective-permute-start.4) | collective-permute-done | bytes 442400 | tf_op jit(solution)/shard_map/ppermute | solution.py:19
  32.2 3.7 %collective-permute-start.5 = (bf16[16,6,18,128]{3,0,2,1:T(8,128)(2,1)S(1)}, bf16[16,6,18,128]{3,0,2,1:T(8,128)(2,1)S(1)}, u32[]{:S(2)}, u32[]{:S(2)}) collective-permute-start(bf16[16,6,18,128]{3,0,2,1:T(8,128)(2,1)S(1)} %collective-permute-done.4), channel_id=1, source_target_pairs={{0,1},{1,2},{2,3},{3,4},{4,5},{5,6},{6,7},{7,0},{8,9},{9,10},{10,1... | collective-permute-start | bytes 1327112 | tf_op jit(solution)/shard_map/ppermute | solution.py:19
  35.9 0.0 collective-permute-start.8
  35.9 5.2 %collective-permute-done.5 = bf16[16,6,18,128]{3,0,2,1:T(8,128)(2,1)S(1)} collective-permute-done((bf16[16,6,18,128]{3,0,2,1:T(8,128)(2,1)S(1)}, bf16[16,6,18,128]{3,0,2,1:T(8,128)(2,1)S(1)}, u32[]{:S(2)}, u32[]{:S(2)}) %collective-permute-start.5) | collective-permute-done | bytes 442400 | tf_op jit(solution)/shard_map/ppermute | solution.py:19
  41.2 3.7 %collective-permute-start.6 = (bf16[16,6,18,128]{3,0,2,1:T(8,128)(2,1)S(1)}, bf16[16,6,18,128]{3,0,2,1:T(8,128)(2,1)S(1)}, u32[]{:S(2)}, u32[]{:S(2)}) collective-permute-start(bf16[16,6,18,128]{3,0,2,1:T(8,128)(2,1)S(1)} %collective-permute-done.5), channel_id=1, source_target_pairs={{0,1},{1,2},{2,3},{3,4},{4,5},{5,6},{6,7},{7,0},{8,9},{9,10},{10,1... | collective-permute-start | bytes 1327112 | tf_op jit(solution)/shard_map/ppermute | solution.py:19
  44.9 0.0 collective-permute-done.8
  44.9 0.0 collective-permute-start.9
  44.9 5.2 %collective-permute-done.6 = bf16[16,6,18,128]{3,0,2,1:T(8,128)(2,1)S(1)} collective-permute-done((bf16[16,6,18,128]{3,0,2,1:T(8,128)(2,1)S(1)}, bf16[16,6,18,128]{3,0,2,1:T(8,128)(2,1)S(1)}, u32[]{:S(2)}, u32[]{:S(2)}) %collective-permute-start.6) | collective-permute-done | bytes 442400 | tf_op jit(solution)/shard_map/ppermute | solution.py:19
  50.1 3.7 %collective-permute-start.7 = (bf16[16,6,18,128]{3,0,2,1:T(8,128)(2,1)S(1)}, bf16[16,6,18,128]{3,0,2,1:T(8,128)(2,1)S(1)}, u32[]{:S(2)}, u32[]{:S(2)}) collective-permute-start(bf16[16,6,18,128]{3,0,2,1:T(8,128)(2,1)S(1)} %collective-permute-done.6), channel_id=1, source_target_pairs={{0,1},{1,2},{2,3},{3,4},{4,5},{5,6},{6,7},{7,0},{8,9},{9,10},{10,1... | collective-permute-start | bytes 1327112 | tf_op jit(solution)/shard_map/ppermute | solution.py:19
  53.8 0.0 copy-start
  53.8 0.0 collective-permute-done.9
  53.8 0.0 collective-permute-start.10
  53.8 5.2 %collective-permute-done.7 = bf16[16,6,18,128]{3,0,2,1:T(8,128)(2,1)S(1)} collective-permute-done((bf16[16,6,18,128]{3,0,2,1:T(8,128)(2,1)S(1)}, bf16[16,6,18,128]{3,0,2,1:T(8,128)(2,1)S(1)}, u32[]{:S(2)}, u32[]{:S(2)}) %collective-permute-start.7) | collective-permute-done | bytes 442400 | tf_op jit(solution)/shard_map/ppermute | solution.py:19
  59.1 0.1 constant_dynamic-update-slice_fusion.17
  59.2 0.1 constant_dynamic-update-slice_fusion.16
  59.3 0.1 constant_dynamic-update-slice_fusion.15
  59.4 0.1 constant_dynamic-update-slice_fusion.14
  59.5 0.1 constant_dynamic-update-slice_fusion.13
  59.6 0.1 constant_dynamic-update-slice_fusion.12
  59.7 3.1 %collective-permute-done.10 = bf16[16,6,18,128]{3,0,2,1:T(8,128)(2,1)S(1)} collective-permute-done((bf16[16,6,18,128]{3,0,2,1:T(8,128)(2,1)S(1)}, bf16[16,6,18,128]{3,0,2,1:T(8,128)(2,1)S(1)}, u32[]{:S(2)}, u32[]{:S(2)}) %collective-permute-start.10) | collective-permute-done | bytes 442400 | tf_op jit(solution)/shard_map/ppermute | solution.py:21
  62.8 0.1 constant_dynamic-update-slice_fusion.11
  62.8 0.1 constant_dynamic-update-slice_fusion.10
  62.9 0.1 constant_dynamic-update-slice_fusion.9
  63.0 0.1 constant_dynamic-update-slice_fusion.8
  63.1 0.1 constant_dynamic-update-slice_fusion.7
  63.2 0.1 constant_dynamic-update-slice_fusion.6
  63.3 0.1 constant_dynamic-update-slice_fusion.5
  63.4 0.1 constant_dynamic-update-slice_fusion.4
  63.5 0.1 constant_dynamic-update-slice_fusion.3
  63.6 0.0 copy-done
  63.6 0.8 %convolution_bitcast_fusion.2 = f32[3,3,16,4,18,128]{5,2,1,0,4,3:T(8,128)S(1)} fusion(bf16[256,6,18,128]{3,0,2,1:T(8,128)(2,1)S(1)} %constant_dynamic-update-slice_fusion.3, s32[]{:T(128)S(6)} %select_n.18, bf16[3,3,3,16,128]{4,3,2,1,0:T(8,128)(2,1)S(1)} %copy-done), kind=kOutput, calls=%fused_computation.2 | convolution fusion | flops 339738624 | bytes 7704580 | tf_op jit(solution)/shard_map/dot_general | solution.py:55
  64.4 0.8 %convolution_bitcast_fusion.1 = f32[3,3,16,4,18,128]{5,2,4,3,1,0:T(8,128)S(1)} fusion(bf16[256,6,18,128]{3,0,2,1:T(8,128)(2,1)S(1)} %constant_dynamic-update-slice_fusion.3, s32[]{:T(128)S(6)} %select_n.18, s32[]{:T(128)S(6)} %add.164, bf16[3,3,3,16,128]{4,3,2,1,0:T(8,128)(2,1)S(1)} %copy-done), kind=kOutput, calls=%fused_computation.1 | convolution fusion | flops 339738624 | bytes 7704584 | tf_op jit(solution)/shard_map/dot_general | solution.py:55
  65.3 0.8 %convolution_bitcast_fusion = f32[3,3,16,4,18,128]{5,2,4,3,1,0:T(8,128)S(1)} fusion(bf16[256,6,18,128]{3,0,2,1:T(8,128)(2,1)S(1)} %constant_dynamic-update-slice_fusion.3, s32[]{:T(128)S(6)} %select_n.18, s32[]{:T(128)S(6)} %add.165, bf16[3,3,3,16,128]{4,3,2,1,0:T(8,128)(2,1)S(1)} %copy-done), kind=kOutput, calls=%fused_computation | convolution fusion | flops 339738624 | bytes 7704584 | tf_op jit(solution)/shard_map/dot_general | solution.py:55
  66.1 0.0 copy-start.1
  66.2 0.3 fusion.2
  66.5 0.3 fusion.8
  66.8 0.2 slice.188
  67.0 0.0 copy-done.1
  67.0 0.4 fusion
  67.4 0.8 %copy.21 = bf16[16,4,16,128]{3,2,1,0:T(8,128)(2,1)} copy(bf16[16,4,16,128]{3,0,2,1:T(8,128)(2,1)S(1)} %fusion) | data formatting | bytes 524288 | tf_op jit(solution)/shard_map/convert_element_type | solution.py:72
  (6 shorter events, 0.1 us)
Async XLA Ops:
  0.9 14.2 %collective-permute-start = (bf16[16,1,16,128]{3,0,2,1:T(8,128)(2,1)S(1)}, bf16[16,1,16,128]{3,0,2,1:T(8,128)(2,1)S(1)}, u32[]{:S(2)}, u32[]{:S(2)}) collective-permute-start(bf16[16,1,16,128]{3,0,2,1:T(8,128)(2,1)S(1)} %copy.37), channel_id=1, source_target_pairs={{0,16},{16,32},{32,48},{48,64},{64,80},{80,96},{96,112},{112,128},... | collective-permute-start | bytes 196616 | tf_op jit(solution)/shard_map/ppermute | solution.py:36
  4.9 12.9 %collective-permute-start.1 = (bf16[16,1,16,128]{3,0,2,1:T(8,128)(2,1)S(1)}, bf16[16,1,16,128]{3,0,2,1:T(8,128)(2,1)S(1)}, u32[]{:S(2)}, u32[]{:S(2)}) collective-permute-start(bf16[16,1,16,128]{3,0,2,1:T(8,128)(2,1)S(1)} %copy.38), channel_id=1, source_target_pairs={{16,0},{32,16},{48,32},{64,48},{80,64},{96,80},{112,96},{128,112},... | collective-permute-start | bytes 196616 | tf_op jit(solution)/shard_map/ppermute | solution.py:37
  17.9 2.6 %collective-permute-start.2 = (bf16[16,6,1,128]{3,0,2,1:T(8,128)(2,1)S(1)}, bf16[16,6,1,128]{3,0,2,1:T(8,128)(2,1)S(1)}, u32[]{:S(2)}, u32[]{:S(2)}) collective-permute-start(bf16[16,6,1,128]{3,0,2,1:T(8,128)(2,1)S(1)} %get-tuple-element.5), channel_id=1, source_target_pairs={{0,8},{1,9},{2,10},{3,11},{4,12},{5,13},{6,14},{7,15},{16,24},{17,... | collective-permute-start | bytes 73736 | tf_op jit(solution)/shard_map/ppermute | solution.py:36
  19.2 4.6 %collective-permute-start.3 = (bf16[16,6,1,128]{3,0,2,1:T(8,128)(2,1)S(1)}, bf16[16,6,1,128]{3,0,2,1:T(8,128)(2,1)S(1)}, u32[]{:S(2)}, u32[]{:S(2)}) collective-permute-start(bf16[16,6,1,128]{3,0,2,1:T(8,128)(2,1)S(1)} %get-tuple-element.6), channel_id=1, source_target_pairs={{8,0},{9,1},{10,2},{11,3},{12,4},{13,5},{14,6},{15,7},{24,16},{25,... | collective-permute-start | bytes 73736 | tf_op jit(solution)/shard_map/ppermute | solution.py:37
  23.8 8.4 %collective-permute-start.4 = (bf16[16,6,18,128]{3,0,2,1:T(8,128)(2,1)S(1)}, bf16[16,6,18,128]{3,0,2,1:T(8,128)(2,1)S(1)}, u32[]{:S(2)}, u32[]{:S(2)}) collective-permute-start(bf16[16,6,18,128]{3,0,2,1:T(8,128)(2,1)S(1)} %pad_maximum_fusion), channel_id=1, source_target_pairs={{0,1},{1,2},{2,3},{3,4},{4,5},{5,6},{6,7},{7,0},{8,9},{9,10},{10,1... | collective-permute-start | bytes 1327112 | tf_op jit(solution)/shard_map/ppermute | solution.py:19
  32.2 8.9 %collective-permute-start.5 = (bf16[16,6,18,128]{3,0,2,1:T(8,128)(2,1)S(1)}, bf16[16,6,18,128]{3,0,2,1:T(8,128)(2,1)S(1)}, u32[]{:S(2)}, u32[]{:S(2)}) collective-permute-start(bf16[16,6,18,128]{3,0,2,1:T(8,128)(2,1)S(1)} %collective-permute-done.4), channel_id=1, source_target_pairs={{0,1},{1,2},{2,3},{3,4},{4,5},{5,6},{6,7},{7,0},{8,9},{9,10},{10,1... | collective-permute-start | bytes 1327112 | tf_op jit(solution)/shard_map/ppermute | solution.py:19
  35.9 8.9 %collective-permute-start.8 = (bf16[16,6,18,128]{3,0,2,1:T(8,128)(2,1)S(1)}, bf16[16,6,18,128]{3,0,2,1:T(8,128)(2,1)S(1)}, u32[]{:S(2)}, u32[]{:S(2)}) collective-permute-start(bf16[16,6,18,128]{3,0,2,1:T(8,128)(2,1)S(1)} %pad_maximum_fusion), channel_id=1, source_target_pairs={{0,7},{1,0},{2,1},{3,2},{4,3},{5,4},{6,5},{7,6},{8,15},{9,8},{10,9... | collective-permute-start | bytes 1327112 | tf_op jit(solution)/shard_map/ppermute | solution.py:21
  41.2 8.9 %collective-permute-start.6 = (bf16[16,6,18,128]{3,0,2,1:T(8,128)(2,1)S(1)}, bf16[16,6,18,128]{3,0,2,1:T(8,128)(2,1)S(1)}, u32[]{:S(2)}, u32[]{:S(2)}) collective-permute-start(bf16[16,6,18,128]{3,0,2,1:T(8,128)(2,1)S(1)} %collective-permute-done.5), channel_id=1, source_target_pairs={{0,1},{1,2},{2,3},{3,4},{4,5},{5,6},{6,7},{7,0},{8,9},{9,10},{10,1... | collective-permute-start | bytes 1327112 | tf_op jit(solution)/shard_map/ppermute | solution.py:19
  44.9 8.9 %collective-permute-start.9 = (bf16[16,6,18,128]{3,0,2,1:T(8,128)(2,1)S(1)}, bf16[16,6,18,128]{3,0,2,1:T(8,128)(2,1)S(1)}, u32[]{:S(2)}, u32[]{:S(2)}) collective-permute-start(bf16[16,6,18,128]{3,0,2,1:T(8,128)(2,1)S(1)} %collective-permute-done.8), channel_id=1, source_target_pairs={{0,7},{1,0},{2,1},{3,2},{4,3},{5,4},{6,5},{7,6},{8,15},{9,8},{10,9... | collective-permute-start | bytes 1327112 | tf_op jit(solution)/shard_map/ppermute | solution.py:21
  50.1 8.9 %collective-permute-start.7 = (bf16[16,6,18,128]{3,0,2,1:T(8,128)(2,1)S(1)}, bf16[16,6,18,128]{3,0,2,1:T(8,128)(2,1)S(1)}, u32[]{:S(2)}, u32[]{:S(2)}) collective-permute-start(bf16[16,6,18,128]{3,0,2,1:T(8,128)(2,1)S(1)} %collective-permute-done.6), channel_id=1, source_target_pairs={{0,1},{1,2},{2,3},{3,4},{4,5},{5,6},{6,7},{7,0},{8,9},{9,10},{10,1... | collective-permute-start | bytes 1327112 | tf_op jit(solution)/shard_map/ppermute | solution.py:19
  53.8 9.8 %copy-start = (bf16[3,3,3,16,128]{4,3,2,1,0:T(8,128)(2,1)S(1)}, bf16[3,3,3,16,128]{4,3,2,1,0:T(8,128)(2,1)}, u32[]{:S(2)}) copy-start(bf16[3,3,3,16,128]{4,3,2,1,0:T(8,128)(2,1)} %param.4) | copy-start | bytes 331780
  53.8 8.9 %collective-permute-start.10 = (bf16[16,6,18,128]{3,0,2,1:T(8,128)(2,1)S(1)}, bf16[16,6,18,128]{3,0,2,1:T(8,128)(2,1)S(1)}, u32[]{:S(2)}, u32[]{:S(2)}) collective-permute-start(bf16[16,6,18,128]{3,0,2,1:T(8,128)(2,1)S(1)} %collective-permute-done.9), channel_id=1, source_target_pairs={{0,7},{1,0},{2,1},{3,2},{4,3},{5,4},{6,5},{7,6},{8,15},{9,8},{10,9... | collective-permute-start | bytes 1327112 | tf_op jit(solution)/shard_map/ppermute | solution.py:21
  66.1 0.8 %copy-start.1 = (f32[16]{0:T(128)S(1)}, f32[16]{0:T(128)}, u32[]{:S(2)}) copy-start(f32[16]{0:T(128)} %param.5) | copy-start | bytes 196
